TPU v7x, 32 devices: a whole 2x2x4 slice. The times are simulated.
32 devices in a mesh: dp: 16 (over z, y, x), rep: 2 (over core).
Axes of the slice: x: 2, y: 2, z: 4, core: 2. Of those that a mesh axis runs over, the one named last changes fastest.
Arguments:
- hidden_old: bfloat16 [8192, 6144], P(('dp', 'rep')), may hold values from -400 to 400
- cotangent: bfloat16 [8192, 128], P(('dp', 'rep')), may hold values from -0.15625 to 0.15625
- gain_old: float32 [6144], replicated, may hold values from 0.1 to 1.9
- old_bounds: int32 [17], replicated, may hold values from 0 to 6144, as said below
- new_bounds: int32 [17], replicated, may hold values from 0 to 8192, as said below
- source_map: int32 [8192], replicated, may hold values from 0 to 6143, as said below
- weight_old: bfloat16 [8192, 128], P('dp'), may hold values from -0.078125 to 0.078125
- moment_first: float32 [8192, 128], P('dp'), may hold values from -6 to 6
- moment_second: float32 [8192, 128], P('dp'), may hold values from 0.25 to 4
Outputs:
- projected: bfloat16 [8192, 128], P(('dp', 'rep'))
- gain_grad: float32 [8192], replicated
- first_next: float32 [10240, 128], P('dp')
- second_next: float32 [10240, 128], P('dp')
- adam_step: float32 [10240, 128], P('dp')
Inputs may be any that keep to these rules, and one draw needn't show every extreme that they name: old_bounds[0] = 0, old_bounds[16] = 6144; device p holds old units old_bounds[p] to old_bounds[p+1] - 1, between 256 and 512 of them, exactly 512 on some device. new_bounds[0] = 0, new_bounds[16] = 8192; device q holds new units new_bounds[q] to new_bounds[q+1] - 1, between 384 and 640 of them, exactly 640 on some device. `source_map`: the s-th new unit of a device (counted from its first) copies an old unit held by old device (s + c) mod 16, with an offset c of that new device; so at most 40 new units of one device copy units of one old device, and some pair of devices reaches 40.
All inputs are finite; a program needn't handle non-finite values.
Results may differ from a plain program's by a relative error of at most 0.0049.
Values may be sent and summed in bfloat16 or wider, within the bound.
No kernel may reach another device: no remote copies, remote signals or barrier semaphores. Data moves between devices by JAX's collectives and lax.ppermute only.
A program may use at most 64 MiB of HBM per device.

v0:
```python
import jax
import jax.numpy as jnp
from jax import lax
from jax.sharding import PartitionSpec as P

D_OLD = 6144
D_NEW = 8192


def owners(bounds, unit_ids):
    return jnp.sum((bounds[None, 1:] <= unit_ids[:, None]).astype(jnp.int32), axis=1)


def routing(
    owner_of,
    local_of,
    table_rows,
    slot_cap,
    dev_index,
    dest_owner,
    new_bounds,
    positions,
    wanted,
    own_slots,
    dp_count,
):
    from_me = (owner_of == dev_index).astype(jnp.int32)
    before = jnp.cumsum(from_me) - from_me
    send_slot = before - before[new_bounds[dest_owner]]
    target = jnp.where(from_me > 0, dest_owner * slot_cap + send_slot, dp_count * slot_cap)
    chosen = jnp.zeros((dp_count * slot_cap,), jnp.int32).at[target].set(positions, mode="drop")
    filled = jnp.zeros((dp_count * slot_cap,), jnp.bool_).at[target].set(True, mode="drop")
    local_row = jnp.clip(local_of[chosen], 0, table_rows - 1)
    anchor = owner_of[wanted]
    earlier = (own_slots[None, :] < own_slots[:, None]) & (anchor[None, :] == anchor[:, None])
    arrival_rank = jnp.sum(earlier.astype(jnp.int32), axis=1)
    incoming = jnp.minimum(anchor * slot_cap + arrival_rank, dp_count * slot_cap - 1)
    return (local_row, filled, incoming)


def outgoing(source_table, route_info):
    return jnp.where(
        route_info[1][:, None], source_table[route_info[0]], jnp.zeros((), source_table.dtype)
    )


def arrived(source_table, route_info, live_new):
    return jnp.where(live_new[:, None], source_table[route_info[2]], 0.0)


def on_device(
    hidden_old,
    cotangent,
    gain_old,
    old_bounds,
    new_bounds,
    source_map,
    weight_old,
    moment_first,
    moment_second,
):
    dp_count = lax.axis_size("dp")
    dev_index = lax.axis_index("dp")
    old_cap = weight_old.shape[0]
    new_mean = D_NEW // dp_count
    new_cap = new_mean + new_mean // 4
    pair_cap = (new_cap + dp_count - 1) // dp_count
    positions = jnp.arange(D_NEW, dtype=jnp.int32)
    first_use = jnp.full((D_OLD,), D_NEW, jnp.int32).at[source_map].min(positions)
    unit_used = first_use < D_NEW
    keep_mask = first_use[source_map] == positions
    copies = jnp.zeros((D_OLD,), jnp.float32).at[source_map].add(1.0)
    padded = jnp.arange(dp_count * old_cap, dtype=jnp.int32)
    slot_owner = padded // old_cap
    within = padded - slot_owner * old_cap
    live_old = within < old_bounds[slot_owner + 1] - old_bounds[slot_owner]
    slot_unit = jnp.minimum(old_bounds[slot_owner] + within, D_OLD - 1)
    weight_live = live_old & unit_used[slot_unit]
    source_owner = owners(old_bounds, source_map)
    source_slot = source_owner * old_cap + source_map - old_bounds[source_owner]
    dest_owner = owners(new_bounds, positions)
    own_slots = jnp.arange(new_cap, dtype=jnp.int32)
    live_new = own_slots < new_bounds[dev_index + 1] - new_bounds[dev_index]
    wanted = jnp.minimum(new_bounds[dev_index] + own_slots, D_NEW - 1)
    grad_route = routing(
        source_owner,
        source_map - old_bounds[dev_index],
        old_cap,
        pair_cap,
        dev_index,
        dest_owner,
        new_bounds,
        positions,
        wanted,
        own_slots,
        dp_count,
    )
    moment_route = routing(
        source_owner,
        source_map - old_bounds[dev_index],
        old_cap,
        pair_cap,
        dev_index,
        dest_owner,
        new_bounds,
        positions,
        wanted,
        own_slots,
        dp_count,
    )
    stream = hidden_old.astype(jnp.float32)
    squares = jnp.sum(stream * stream * copies, axis=1)
    inv_rms = lax.rsqrt(squares / D_NEW + 1e-05)
    normed = (stream * inv_rms[:, None] * gain_old).astype(jnp.bfloat16)
    normed_slots = jnp.take(normed, slot_unit, axis=1)
    hidden_slots = jnp.take(hidden_old, slot_unit, axis=1)
    weight_block = lax.all_gather(weight_old, "dp", axis=0, tiled=True)
    masked_block = jnp.where(weight_live[:, None], weight_block, jnp.zeros((), weight_block.dtype))
    columns = normed_slots
    key_sums = jnp.dot(columns, masked_block, preferred_element_type=jnp.float32)
    slopes = lax.dot_general(
        cotangent, masked_block, (((1,), (1,)), ((), ())), preferred_element_type=jnp.float32
    )
    scaled = hidden_slots.astype(jnp.float32) * inv_rms[:, None]
    column_terms = jnp.sum(slopes * scaled, axis=0)
    key_sums, column_terms = (key_sums, column_terms)
    projected = key_sums.astype(jnp.bfloat16)
    columns = normed_slots
    grad_own = lax.psum_scatter(
        lax.dot_general(
            columns, cotangent, (((0,), (0,)), ((), ())), preferred_element_type=jnp.float32
        ),
        "dp",
        scatter_dimension=0,
        tiled=True,
    )
    grad_own = lax.psum(grad_own.astype(jnp.bfloat16), "rep").astype(jnp.float32)
    column_total = lax.psum(column_terms, ("dp", "rep"))
    gain_grad = jnp.where(keep_mask, column_total[source_slot], 0.0)
    moved_grad, moved_first, moved_second = (
        lax.all_to_all(
            outgoing(grad_own, grad_route), "dp", split_axis=0, concat_axis=0, tiled=True
        ),
        lax.all_to_all(
            outgoing(moment_first, moment_route), "dp", split_axis=0, concat_axis=0, tiled=True
        ),
        lax.all_to_all(
            outgoing(moment_second, moment_route), "dp", split_axis=0, concat_axis=0, tiled=True
        ),
    )
    grad_new = arrived(moved_grad, grad_route, live_new)
    first_next = jnp.where(
        live_new[:, None], 0.9 * arrived(moved_first, moment_route, live_new) + 0.1 * grad_new, 0.0
    )
    second_next = jnp.where(
        live_new[:, None],
        0.95 * arrived(moved_second, moment_route, live_new) + 0.05 * grad_new * grad_new,
        0.0,
    )
    adam_step = first_next / (jnp.sqrt(second_next) + 1e-08)
    return (projected, gain_grad, first_next, second_next, adam_step)


def solution(mesh):
    placed = (
        P(("dp", "rep"), None),
        P(("dp", "rep"), None),
        P(),
        P(),
        P(),
        P(),
        P("dp", None),
        P("dp", None),
        P("dp", None),
    )
    return jax.shard_map(
        on_device,
        mesh=mesh,
        in_specs=placed,
        out_specs=(P(("dp", "rep"), None), P(), P("dp", None), P("dp", None), P("dp", None)),
        check_vma=False,
    )
```

profile of v0, /device:TPU:0, one launch (start us, length us, event | category | flops | bytes accessed | tf_op | source)
XLA Modules:
  0.0 749.6 jit_solution(12491640202311818620)
XLA Ops:
  7.8 2.0 fusion.43
  9.9 4.5 compare_select_fusion.25
  14.4 6.3 compare_and_fusion
  20.7 3.2 copy.20
  23.9 1.3 broadcast_subtract_fusion
  25.8 44.6 %scatter_custom_fusion = f32[6144]{0:T(1024)} fusion(s32[8192]{0:T(1024)} %get-tuple-element.42, f32[8192]{0:T(1024)} %broadcast.609, f32[]{:T(128)} %constant.37.clone.1), kind=kCustom, calls=%fused_computation.165 | custom fusion | flops 8192 | bytes 25088 | tf_op jit(solution)/shard_map/scatter-add | solution.py:72
  70.5 1.7 fusion.2
  72.2 2.9 fusion.4
  75.0 33.2 %gather_fusion.12 = bf16[8192,256]{1,0:T(8,128)(2,1)} fusion(bf16[256,6144]{0,1:T(8,128)(2,1)} %fusion.4, s32[8192]{0:T(1024)S(1)} %broadcast_clamp_fusion.3), kind=kCustom, calls=%fused_computation.clone | custom fusion | bytes 8421376 | tf_op jit(solution)/shard_map/jit(_take)/gather | solution.py:115
  108.2 7.2 fusion.5
  115.5 98.0 %reduce-scatter.2.cloned.1.call-done = f32[512,128]{1,0:T(8,128)} async-done(((f32[8192,128]{1,0:T(8,128)}), f32[512,128]{1,0:T(8,128)}) %reduce-scatter.2.cloned.1.call-update) | async-done | bytes 262160 | tf_op jit(solution)/shard_map/reduce_scatter | solution.py:129
  213.5 1.6 convert_element_type.58
  215.1 0.7 all-gather.2.cloned.1.call-update
  217.1 0.7 fusion.42
  218.0 4.5 compare_select_fusion.7
  222.6 1.0 compare_reduce_fusion.9
  223.5 6.2 select_select_fusion
  230.5 0.8 convert_reduce_fusion.2
  231.9 1.0 reduce-window.9
  233.0 0.7 slice.117
  233.7 1.4 reduce-window.12
  235.1 0.9 slice_reduce_fusion
  236.0 1.5 convert_subtract_fusion
  237.4 80.7 %gather_fusion.3 = s32[8192]{0:T(1024)} fusion(s32[8192]{0:T(1024)S(1)} %get-tuple-element.31, s32[8192]{0:T(1024)} %broadcast_clamp_fusion), kind=kCustom, calls=%fused_computation.5 | custom fusion | bytes 98304 | tf_op jit(solution)/shard_map/gather | solution.py:29
  318.1 6.1 compare_select_fusion.13
  324.2 30.8 %scatter_custom_fusion.3 = s32[640]{0:T(1024)S(1)} fusion(s32[8192]{0:T(1024)} %bitcast.97, s32[8192]{0:T(1024)S(1)} %iota.49, s32[]{:T(128)} %constant.38.clone.1), kind=kCustom, calls=%fused_computation.178 | custom fusion | bytes 3072 | tf_op jit(solution)/shard_map/scatter | solution.py:31
  355.1 3.9 gather_fusion.4
  359.0 2.3 gather_fusion.5
  361.2 3.2 gather_fusion.10
  364.5 34.7 %scatter_custom_fusion.2 = pred[640]{0:T(1024)(128)(4,1)S(1)} fusion(s32[8192]{0:T(1024)} %bitcast.98, pred[8192]{0:T(1024)(128)(4,1)S(1)} %broadcast.610, pred[]{:T(512)} %constant.95.clone.1), kind=kCustom, calls=%fused_computation.180 | custom fusion | bytes 1152 | tf_op jit(solution)/shard_map/scatter | solution.py:32
  399.2 0.7 broadcast_in_dim.153
  399.9 0.7 fusion.31
  400.6 3.9 gather_fusion.6
  406.4 44.3 %scatter_custom_fusion.1 = s32[6144]{0:T(1024)S(1)} fusion(s32[8192]{0:T(1024)} %get-tuple-element.42, s32[8192]{0:T(1024)} %iota.45, s32[]{:T(128)} %constant.34.clone.1), kind=kCustom, calls=%fused_computation.163 | custom fusion | flops 8192 | bytes 25088 | tf_op jit(solution)/shard_map/scatter-min | solution.py:69
  451.0 0.7 compare_reduce_fusion.20
  451.7 0.6 compare_reduce_fusion.21
  452.3 0.6 compare_reduce_fusion.22
  453.0 0.6 compare_reduce_fusion.23
  453.6 0.6 compare_reduce_fusion.24
  454.3 0.6 compare_reduce_fusion.25
  454.9 0.6 compare_reduce_fusion.26
  456.2 0.6 compare_reduce_fusion.28
  458.2 1.6 convert_element_type.59
  459.8 3.2 gather_fusion.8
  463.0 2.3 broadcast_select_fusion.8
  465.2 5.2 all-to-all-start.2
  470.5 0.6 compare_reduce_fusion.29
  471.1 32.9 %gather_fusion.13 = bf16[8192,256]{1,0:T(8,128)(2,1)} fusion(bf16[256,6144]{0,1:T(8,128)(2,1)S(1)} %copy.20, s32[8192]{0:T(1024)S(1)} %copy-done.6), kind=kCustom, calls=%fused_computation.1.clone | custom fusion | bytes 8421376 | tf_op jit(solution)/shard_map/jit(_take)/gather | solution.py:116
  504.1 6.4 copy.22
  510.5 45.5 %gather_fusion.1 = s32[8192]{0:T(1024)S(1)} fusion(s32[6144]{0:T(1024)S(1)} %scatter_custom_fusion.1, s32[8192]{0:T(1024)S(1)} %copy-done.13), kind=kCustom, calls=%fused_computation.3 | custom fusion | bytes 98304 | tf_op jit(solution)/shard_map/gather | solution.py:71
  556.2 50.7 %gather_fusion = pred[8192]{0:T(1024)(128)(4,1)S(1)} fusion(pred[6144]{0:T(1024)(128)(4,1)S(1)} %broadcast_compare_fusion.1, s32[8192]{0:T(1024)S(1)} %copy-done.9), kind=kCustom, calls=%fused_computation.2 | custom fusion | bytes 49152 | tf_op jit(solution)/shard_map/gather | solution.py:78
  606.9 1.0 compare_reduce_fusion.19
  608.0 6.3 fusion.25
  614.3 6.3 fusion.22
  620.7 6.9 all-to-all-start
  627.6 7.3 fusion.9
  635.0 40.8 %psum.14 = f32[8192]{0:T(1024)S(1)} all-reduce(f32[8192]{0:T(1024)S(1)} %fusion.9), channel_id=1, replica_groups=mesh['dp'=16,'rep'=2] {'dp','rep'}, use_global_device_ids=true, to_apply=%region_4.6 | all-reduce | flops 8192 | bytes 65536 | tf_op jit(solution)/shard_map/psum | solution.py:138
  675.8 45.5 %gather_fusion.2 = f32[8192]{0:T(1024)S(1)} fusion(f32[8192]{0:T(1024)S(1)} %psum.14, s32[8192]{0:T(1024)S(1)} %fusion.22), kind=kCustom, calls=%fused_computation.4 | custom fusion | bytes 98304 | tf_op jit(solution)/shard_map/gather | solution.py:139
  721.4 5.4 all-to-all-start.1
  727.4 8.4 %fusion.11 = bf16[256,128]{1,0:T(8,128)(2,1)} fusion(bf16[8192,256]{1,0:T(8,128)(2,1)} %gather_fusion.12, pred[8192]{0:T(1024)(128)(4,1)S(1)} %get-tuple-element.37, bf16[8192,128]{1,0:T(8,128)(2,1)S(1)} %copy-done.28, pred[8192]{0:T(1024)(128)(4,1)S(1)} %fusion.25), kind=kOutput, calls=%fused_computation.36 | convolution fusion | flops 540049408 | bytes 6373376 | tf_op jit(solution)/shard_map/dot_general | solution.py:120
  735.8 2.6 gather_fusion.11
  738.4 1.7 gather_fusion.7
  740.1 1.7 gather_fusion.9
  741.8 1.2 add_divide_fusion
  (107 shorter events, 7.8 us)
Async XLA Ops:
  7.2 351.8 %copy-start = (f32[512,128]{1,0:T(8,128)S(1)}, f32[512,128]{1,0:T(8,128)}, u32[]{:S(2)}) copy-start(f32[512,128]{1,0:T(8,128)} %param.18) | copy-start | bytes 786436
  7.2 16.8 %copy-start.2 = (s32[8192]{0:T(1024)S(1)}, s32[8192]{0:T(1024)}, u32[]{:S(2)}) copy-start(s32[8192]{0:T(1024)} %param.16) | copy-start | bytes 98308
  7.2 206.3 %reduce-scatter.2.cloned.1.call-start = ((), (), s32[]{:S(2)}) async-start(), calls=%async_computation.5 | async-start | bytes 4456448 | tf_op jit(solution)/shard_map/reduce_scatter | solution.py:129
  20.7 54.3 %copy-start.5 = (s32[8192]{0:T(1024)}, s32[8192]{0:T(1024)S(1)}, u32[]{:S(2)}) copy-start(s32[8192]{0:T(1024)S(1)} %broadcast_clamp_fusion.3) | copy-start | bytes 98308
  72.2 36.1 %copy-start.25 = (f32[256]{0:T(256)}, f32[256]{0:T(256)S(1)}, u32[]{:S(2)}) copy-start(f32[256]{0:T(256)S(1)} %add_rsqrt_fusion) | copy-start | bytes 3076
  115.4 100.4 %copy-start.8 = (s32[17]{0:T(128)S(1)}, s32[17]{0:T(128)}, u32[]{:S(2)}) copy-start(s32[17]{0:T(128)} %param.15) | copy-start | bytes 208
  115.4 101.1 %copy-start.7 = (s32[17]{0:T(128)S(1)}, s32[17]{0:T(128)}, u32[]{:S(2)}) copy-start(s32[17]{0:T(128)} %param.14) | copy-start | bytes 208
  115.4 342.7 %all-reduce.2.cloned.1.call-start = ((), (), s32[]{:S(2)}) async-start(), calls=%async_computation.6 | async-start | bytes 262144 | tf_op jit(solution)/shard_map/psum | solution.py:137
  215.1 412.5 %all-gather.2.cloned.1.call-start = ((), (), s32[]{:S(2)}) async-start(), calls=%async_computation.4 | async-start | bytes 2228224 | tf_op jit(solution)/shard_map/all_gather | solution.py:117
  218.0 11.8 %copy-start.4 = (s32[8192]{0:T(1024)}, s32[8192]{0:T(1024)S(1)}, u32[]{:S(2)}) copy-start(s32[8192]{0:T(1024)S(1)} %convert_reduce_fusion.1) | copy-start | bytes 98308
  233.0 3.0 copy-start.1
  404.4 66.7 %copy-start.6 = (s32[8192]{0:T(1024)S(1)}, s32[8192]{0:T(1024)}, u32[]{:S(2)}) copy-start(s32[8192]{0:T(1024)} %copy-done.5) | copy-start | bytes 98308
  465.2 155.4 %all-to-all-start.2 = ((f32[16,40,128]{2,1,0:T(8,128)}), f32[16,40,128]{2,1,0:T(8,128)}, u32[]{:S(2)}, u32[]{:S(2)}) async-start(f32[16,40,128]{2,1,0:T(8,128)} %get-tuple-element.45), calls=%async_computation.3 | async-start | bytes 655360 | tf_op jit(solution)/shard_map/all_to_all | solution.py:147
  504.1 6.4 copy-start.13
  510.4 45.5 %copy-start.9 = (s32[8192]{0:T(1024)S(1)}, s32[8192]{0:T(1024)}, u32[]{:S(2)}) copy-start(s32[8192]{0:T(1024)} %broadcast_clamp_fusion.2) | copy-start | bytes 98308
  556.0 50.9 %copy-start.10 = (s32[8192,1]{0,1:T(1,128)S(1)}, s32[8192,1]{0,1:T(1,128)}, u32[]{:S(2)}) copy-start(s32[8192,1]{0,1:T(1,128)} %get-tuple-element.36) | copy-start | bytes 98308
  556.0 51.9 %copy-start.12 = (s32[8192,1]{0,1:T(1,128)S(1)}, s32[8192,1]{0,1:T(1,128)}, u32[]{:S(2)}) copy-start(s32[8192,1]{0,1:T(1,128)} %get-tuple-element.82) | copy-start | bytes 98308
  556.0 51.9 %copy-start.15 = (pred[8192]{0:T(1024)(128)(4,1)S(1)}, pred[8192]{0:T(1024)(128)(4,1)}, u32[]{:S(2)}) copy-start(pred[8192]{0:T(1024)(128)(4,1)} %compare_reduce_fusion.20) | copy-start | bytes 24580
  556.0 51.9 %copy-start.16 = (pred[8192]{0:T(1024)(128)(4,1)S(1)}, pred[8192]{0:T(1024)(128)(4,1)}, u32[]{:S(2)}) copy-start(pred[8192]{0:T(1024)(128)(4,1)} %compare_reduce_fusion.21) | copy-start | bytes 24580
  556.0 51.9 %copy-start.17 = (pred[8192]{0:T(1024)(128)(4,1)S(1)}, pred[8192]{0:T(1024)(128)(4,1)}, u32[]{:S(2)}) copy-start(pred[8192]{0:T(1024)(128)(4,1)} %compare_reduce_fusion.22) | copy-start | bytes 24580
  556.0 51.9 %copy-start.18 = (pred[8192]{0:T(1024)(128)(4,1)S(1)}, pred[8192]{0:T(1024)(128)(4,1)}, u32[]{:S(2)}) copy-start(pred[8192]{0:T(1024)(128)(4,1)} %compare_reduce_fusion.23) | copy-start | bytes 24580
  556.1 51.9 %copy-start.19 = (pred[8192]{0:T(1024)(128)(4,1)S(1)}, pred[8192]{0:T(1024)(128)(4,1)}, u32[]{:S(2)}) copy-start(pred[8192]{0:T(1024)(128)(4,1)} %compare_reduce_fusion.24) | copy-start | bytes 24580
  556.1 51.9 %copy-start.20 = (pred[8192]{0:T(1024)(128)(4,1)S(1)}, pred[8192]{0:T(1024)(128)(4,1)}, u32[]{:S(2)}) copy-start(pred[8192]{0:T(1024)(128)(4,1)} %compare_reduce_fusion.25) | copy-start | bytes 24580
  556.1 51.9 %copy-start.21 = (pred[8192]{0:T(1024)(128)(4,1)S(1)}, pred[8192]{0:T(1024)(128)(4,1)}, u32[]{:S(2)}) copy-start(pred[8192]{0:T(1024)(128)(4,1)} %compare_reduce_fusion.26) | copy-start | bytes 24580
  556.1 51.9 %copy-start.22 = (pred[8192]{0:T(1024)(128)(4,1)S(1)}, pred[8192]{0:T(1024)(128)(4,1)}, u32[]{:S(2)}) copy-start(pred[8192]{0:T(1024)(128)(4,1)} %compare_reduce_fusion.27) | copy-start | bytes 24580
  556.1 51.9 %copy-start.23 = (pred[8192]{0:T(1024)(128)(4,1)S(1)}, pred[8192]{0:T(1024)(128)(4,1)}, u32[]{:S(2)}) copy-start(pred[8192]{0:T(1024)(128)(4,1)} %compare_reduce_fusion.28) | copy-start | bytes 24580
  556.1 51.9 %copy-start.24 = (pred[8192]{0:T(1024)(128)(4,1)S(1)}, pred[8192]{0:T(1024)(128)(4,1)}, u32[]{:S(2)}) copy-start(pred[8192]{0:T(1024)(128)(4,1)} %compare_reduce_fusion.29) | copy-start | bytes 24580
  556.1 58.2 %copy-start.3 = (s32[8192]{0:T(1024)S(1)}, s32[8192]{0:T(1024)}, u32[]{:S(2)}) copy-start(s32[8192]{0:T(1024)} %param.16) | copy-start | bytes 98308
  556.1 58.2 %copy-start.11 = (s32[8192,1]{0,1:T(1,128)S(1)}, s32[8192,1]{0,1:T(1,128)}, u32[]{:S(2)}) copy-start(s32[8192,1]{0,1:T(1,128)} %get-tuple-element.35) | copy-start | bytes 98308
  556.1 71.5 %copy-start.14 = (bf16[256,128]{1,0:T(8,128)(2,1)S(1)}, bf16[256,128]{1,0:T(8,128)(2,1)}, u32[]{:S(2)}) copy-start(bf16[256,128]{1,0:T(8,128)(2,1)} %param.12) | copy-start | bytes 196612
  556.1 71.5 %copy-start.26 = (f32[256]{0:T(256)S(1)}, f32[256]{0:T(256)}, u32[]{:S(2)}) copy-start(f32[256]{0:T(256)} %copy-done.25) | copy-start | bytes 3076
  620.7 100.7 %all-to-all-start = ((f32[16,40,128]{2,1,0:T(8,128)}), f32[16,40,128]{2,1,0:T(8,128)S(1)}, u32[]{:S(2)}, u32[]{:S(2)}) async-start(f32[16,40,128]{2,1,0:T(8,128)} %get-tuple-element.43), calls=%async_computation | async-start | bytes 655360 | tf_op jit(solution)/shard_map/all_to_all | solution.py:144
  675.8 51.6 %copy-start.28 = (bf16[8192,128]{1,0:T(8,128)(2,1)S(1)}, bf16[8192,128]{1,0:T(8,128)(2,1)}, u32[]{:S(2)}) copy-start(bf16[8192,128]{1,0:T(8,128)(2,1)} %all-gather.2.cloned.1.call-done) | copy-start | bytes 6291460
  721.4 18.7 %all-to-all-start.1 = ((f32[16,40,128]{2,1,0:T(8,128)}), f32[16,40,128]{2,1,0:T(8,128)S(1)}, u32[]{:S(2)}, u32[]{:S(2)}) async-start(f32[16,40,128]{2,1,0:T(8,128)} %get-tuple-element.44), calls=%async_computation.2 | async-start | bytes 655360 | tf_op jit(solution)/shard_map/all_to_all | solution.py:141
  735.8 6.0 copy-start.27
Sparse Core Ops, SparseCore 0:
  115.6 97.8 reduce-scatter.1
  216.3 17.4 all-reduce.1
  236.6 61.8 all-gather.1
where the time goes:
time: 752 us; the launch traced here: 750 us
  local copies, waits for them, and re-layouts  394 us (52%)
  other arithmetic  160 us (21%)
  waiting for transfers between devices  98.7 us (13%)
  blocking collectives  40.8 us (5%)
  matrix products  22.9 us (3%)
  starting transfers between devices  17.7 us (2%)
  between operations  15.8 us (2%)
    reduce_scatter x1, waiting for transfers between devices, on_device(): lax.psum_scatter(lax.dot_general(columns, cotangent, (((0,), (0,)), ((),...  98 us
    gather x2, local copies, waits for them, and re-layouts, routing(): send_slot = before - before[new_bounds[dest_owner]]  81.3 us
    gather x1, local copies, waits for them, and re-layouts, on_device(): weight_live = live_old & unit_used[slot_unit]  50.7 us
    gather x1, local copies, waits for them, and re-layouts, on_device(): gain_grad = jnp.where(keep_mask, column_total[source_slot], 0.0)  45.5 us
    gather x1, local copies, waits for them, and re-layouts, on_device(): keep_mask = first_use[source_map] == positions  45.5 us
    scatter-add x1, other arithmetic, on_device(): copies = jnp.zeros((D_OLD,), jnp.float32).at[source_map].add(1.0)  44.6 us
    another operation x1, other arithmetic, on_device(): jnp.full((D_OLD,), D_NEW, jnp.int32).at[source_map].min(positions)  44.3 us
    psum x1, blocking collectives, on_device(): column_total = lax.psum(column_terms, ('dp', 'rep'))  40.8 us
  transfers between devices with their start and end apart: 6, of which 1 were waited for; matrix products, arithmetic and copies ran while one was open for 62% of the time, Pallas kernels for 0%

commit v1 on v0

--- a/solution.py
+++ b/solution.py
@@ -135,7 +135,7 @@
         tiled=True,
     )
     grad_own = lax.psum(grad_own.astype(jnp.bfloat16), "rep").astype(jnp.float32)
-    column_total = lax.psum(column_terms, ("dp", "rep"))
+    column_total = lax.psum(lax.psum(column_terms, "rep"), "dp")
     gain_grad = jnp.where(keep_mask, column_total[source_slot], 0.0)
     moved_grad, moved_first, moved_second = (
         lax.all_to_all(

time: 752 us -> 790 us (1.051)
  blocking collectives: 40.8 us -> 80.5 us
    psum x1 -> x2, blocking collectives: 40.8 us -> 80.5 us  [on_device(): column_total = lax.psum(lax.psum(column_terms, 'rep'), 'dp')]
  transfers between devices with their start and end apart: 6 -> 6, of which waited for: 1 -> 1; matrix products, arithmetic and copies ran while one was open for 62% -> 59% of each run, Pallas kernels for 0% -> 0%
where the time goes in v1:
time: 790 us; the launch traced here: 787 us
  local copies, waits for them, and re-layouts  394 us (50%)
  other arithmetic  160 us (20%)
  waiting for transfers between devices  98.7 us (12%)
  blocking collectives  80.5 us (10%)
  matrix products  22.9 us (3%)
  starting transfers between devices  15.8 us (2%)
  between operations  15.8 us (2%)
    reduce_scatter x1, waiting for transfers between devices, on_device(): lax.psum_scatter(lax.dot_general(columns, cotangent, (((0,), (0,)), ((),...  98 us
    gather x2, local copies, waits for them, and re-layouts, routing(): send_slot = before - before[new_bounds[dest_owner]]  81.3 us
    psum x2, blocking collectives, on_device(): column_total = lax.psum(lax.psum(column_terms, 'rep'), 'dp')  80.5 us
    gather x1, local copies, waits for them, and re-layouts, on_device(): weight_live = live_old & unit_used[slot_unit]  50.7 us
    gather x1, local copies, waits for them, and re-layouts, on_device(): keep_mask = first_use[source_map] == positions  45.5 us
    gather x1, local copies, waits for them, and re-layouts, on_device(): gain_grad = jnp.where(keep_mask, column_total[source_slot], 0.0)  45.5 us
    scatter-add x1, other arithmetic, on_device(): copies = jnp.zeros((D_OLD,), jnp.float32).at[source_map].add(1.0)  44.6 us
    another operation x1, other arithmetic, on_device(): jnp.full((D_OLD,), D_NEW, jnp.int32).at[source_map].min(positions)  44.3 us
  transfers between devices with their start and end apart: 6, of which 1 were waited for; matrix products, arithmetic and copies ran while one was open for 59% of the time, Pallas kernels for 0%

profile of v1, /device:TPU:0, one launch (start us, length us, event | category | flops | bytes accessed | tf_op | source)
XLA Modules:
  0.0 787.4 jit_solution(10755453295044611267)
XLA Ops:
  7.8 2.0 fusion.43
  9.9 4.5 compare_select_fusion.25
  14.4 6.3 compare_and_fusion
  20.7 3.2 copy.20
  23.9 1.3 broadcast_subtract_fusion
  25.8 44.6 %scatter_custom_fusion = f32[6144]{0:T(1024)} fusion(s32[8192]{0:T(1024)} %get-tuple-element.42, f32[8192]{0:T(1024)} %broadcast.609, f32[]{:T(128)} %constant.37.clone.1), kind=kCustom, calls=%fused_computation.165 | custom fusion | flops 8192 | bytes 25088 | tf_op jit(solution)/shard_map/scatter-add | solution.py:72
  70.5 1.7 fusion.2
  72.2 2.9 fusion.4
  75.0 33.2 %gather_fusion.12 = bf16[8192,256]{1,0:T(8,128)(2,1)} fusion(bf16[256,6144]{0,1:T(8,128)(2,1)} %fusion.4, s32[8192]{0:T(1024)S(1)} %broadcast_clamp_fusion.3), kind=kCustom, calls=%fused_computation.clone | custom fusion | bytes 8421376 | tf_op jit(solution)/shard_map/jit(_take)/gather | solution.py:115
  108.2 7.2 fusion.5
  115.5 98.0 %reduce-scatter.2.cloned.1.call-done = f32[512,128]{1,0:T(8,128)} async-done(((f32[8192,128]{1,0:T(8,128)}), f32[512,128]{1,0:T(8,128)}) %reduce-scatter.2.cloned.1.call-update) | async-done | bytes 262160 | tf_op jit(solution)/shard_map/reduce_scatter | solution.py:129
  213.5 1.6 convert_element_type.58
  215.1 0.7 all-gather.2.cloned.1.call-update
  217.1 0.7 fusion.42
  218.0 4.5 compare_select_fusion.7
  222.6 1.0 compare_reduce_fusion.9
  223.5 6.2 select_select_fusion
  230.5 0.8 convert_reduce_fusion.2
  231.9 1.0 reduce-window.9
  233.0 0.7 slice.117
  233.7 1.4 reduce-window.12
  235.1 0.9 slice_reduce_fusion
  236.0 1.5 convert_subtract_fusion
  237.4 80.7 %gather_fusion.3 = s32[8192]{0:T(1024)} fusion(s32[8192]{0:T(1024)S(1)} %get-tuple-element.31, s32[8192]{0:T(1024)} %broadcast_clamp_fusion), kind=kCustom, calls=%fused_computation.5 | custom fusion | bytes 98304 | tf_op jit(solution)/shard_map/gather | solution.py:29
  318.1 6.1 compare_select_fusion.13
  324.2 30.8 %scatter_custom_fusion.3 = s32[640]{0:T(1024)S(1)} fusion(s32[8192]{0:T(1024)} %bitcast.97, s32[8192]{0:T(1024)S(1)} %iota.49, s32[]{:T(128)} %constant.38.clone.1), kind=kCustom, calls=%fused_computation.178 | custom fusion | bytes 3072 | tf_op jit(solution)/shard_map/scatter | solution.py:31
  355.1 3.9 gather_fusion.4
  359.0 2.3 gather_fusion.5
  361.2 3.2 gather_fusion.10
  364.5 34.7 %scatter_custom_fusion.2 = pred[640]{0:T(1024)(128)(4,1)S(1)} fusion(s32[8192]{0:T(1024)} %bitcast.98, pred[8192]{0:T(1024)(128)(4,1)S(1)} %broadcast.610, pred[]{:T(512)} %constant.95.clone.1), kind=kCustom, calls=%fused_computation.180 | custom fusion | bytes 1152 | tf_op jit(solution)/shard_map/scatter | solution.py:32
  399.2 0.7 broadcast_in_dim.153
  399.9 0.7 fusion.31
  400.6 3.9 gather_fusion.6
  406.4 44.3 %scatter_custom_fusion.1 = s32[6144]{0:T(1024)S(1)} fusion(s32[8192]{0:T(1024)} %get-tuple-element.42, s32[8192]{0:T(1024)} %iota.45, s32[]{:T(128)} %constant.34.clone.1), kind=kCustom, calls=%fused_computation.163 | custom fusion | flops 8192 | bytes 25088 | tf_op jit(solution)/shard_map/scatter-min | solution.py:69
  451.0 0.7 compare_reduce_fusion.20
  451.7 0.6 compare_reduce_fusion.21
  452.3 0.6 compare_reduce_fusion.22
  453.0 0.6 compare_reduce_fusion.23
  454.3 0.6 compare_reduce_fusion.25
  454.9 0.6 compare_reduce_fusion.26
  456.2 0.6 compare_reduce_fusion.28
  458.2 1.6 convert_element_type.59
  459.8 3.2 gather_fusion.8
  463.0 2.3 broadcast_select_fusion.8
  465.2 5.2 all-to-all-start.2
  470.5 0.6 compare_reduce_fusion.29
  471.1 32.9 %gather_fusion.13 = bf16[8192,256]{1,0:T(8,128)(2,1)} fusion(bf16[256,6144]{0,1:T(8,128)(2,1)S(1)} %copy.20, s32[8192]{0:T(1024)S(1)} %copy-done.6), kind=kCustom, calls=%fused_computation.1.clone | custom fusion | bytes 8421376 | tf_op jit(solution)/shard_map/jit(_take)/gather | solution.py:116
  504.1 6.4 copy.22
  510.5 45.5 %gather_fusion.1 = s32[8192]{0:T(1024)S(1)} fusion(s32[6144]{0:T(1024)S(1)} %scatter_custom_fusion.1, s32[8192]{0:T(1024)S(1)} %copy-done.13), kind=kCustom, calls=%fused_computation.3 | custom fusion | bytes 98304 | tf_op jit(solution)/shard_map/gather | solution.py:71
  556.2 50.7 %gather_fusion = pred[8192]{0:T(1024)(128)(4,1)S(1)} fusion(pred[6144]{0:T(1024)(128)(4,1)S(1)} %broadcast_compare_fusion.1, s32[8192]{0:T(1024)S(1)} %copy-done.9), kind=kCustom, calls=%fused_computation.2 | custom fusion | bytes 49152 | tf_op jit(solution)/shard_map/gather | solution.py:78
  606.9 1.0 compare_reduce_fusion.19
  608.0 6.3 fusion.25
  614.3 6.3 fusion.22
  620.7 6.9 all-to-all-start
  627.6 7.3 fusion.9
  635.0 3.4 psum.21
  638.4 77.1 %psum.22 = f32[8192]{0:T(1024)S(1)} all-reduce(f32[8192]{0:T(1024)S(1)} %psum.21), channel_id=1, replica_groups=mesh['dp'=16,'rep'=2] {'dp'}, use_global_device_ids=true, to_apply=%region_5.7 | all-reduce | flops 8192 | bytes 65536 | tf_op jit(solution)/shard_map/psum | solution.py:138
  715.5 45.5 %gather_fusion.2 = f32[8192]{0:T(1024)S(1)} fusion(f32[8192]{0:T(1024)S(1)} %psum.22, s32[8192]{0:T(1024)S(1)} %fusion.22), kind=kCustom, calls=%fused_computation.4 | custom fusion | bytes 98304 | tf_op jit(solution)/shard_map/gather | solution.py:139
  761.1 3.6 all-to-all-start.1
  765.3 8.4 %fusion.11 = bf16[256,128]{1,0:T(8,128)(2,1)} fusion(bf16[8192,256]{1,0:T(8,128)(2,1)} %gather_fusion.12, pred[8192]{0:T(1024)(128)(4,1)S(1)} %get-tuple-element.37, bf16[8192,128]{1,0:T(8,128)(2,1)S(1)} %copy-done.28, pred[8192]{0:T(1024)(128)(4,1)S(1)} %fusion.25), kind=kOutput, calls=%fused_computation.36 | convolution fusion | flops 540049408 | bytes 6373376 | tf_op jit(solution)/shard_map/dot_general | solution.py:120
  773.6 2.6 gather_fusion.11
  776.3 1.7 gather_fusion.7
  777.9 1.7 gather_fusion.9
  779.6 1.2 add_divide_fusion
  (108 shorter events, 8.5 us)
Async XLA Ops:
  7.2 351.8 %copy-start = (f32[512,128]{1,0:T(8,128)S(1)}, f32[512,128]{1,0:T(8,128)}, u32[]{:S(2)}) copy-start(f32[512,128]{1,0:T(8,128)} %param.18) | copy-start | bytes 786436
  7.2 16.8 %copy-start.2 = (s32[8192]{0:T(1024)S(1)}, s32[8192]{0:T(1024)}, u32[]{:S(2)}) copy-start(s32[8192]{0:T(1024)} %param.16) | copy-start | bytes 98308
  7.2 206.3 %reduce-scatter.2.cloned.1.call-start = ((), (), s32[]{:S(2)}) async-start(), calls=%async_computation.5 | async-start | bytes 4456448 | tf_op jit(solution)/shard_map/reduce_scatter | solution.py:129
  20.7 54.3 %copy-start.5 = (s32[8192]{0:T(1024)}, s32[8192]{0:T(1024)S(1)}, u32[]{:S(2)}) copy-start(s32[8192]{0:T(1024)S(1)} %broadcast_clamp_fusion.3) | copy-start | bytes 98308
  72.2 36.1 %copy-start.25 = (f32[256]{0:T(256)}, f32[256]{0:T(256)S(1)}, u32[]{:S(2)}) copy-start(f32[256]{0:T(256)S(1)} %add_rsqrt_fusion) | copy-start | bytes 3076
  115.4 100.4 %copy-start.8 = (s32[17]{0:T(128)S(1)}, s32[17]{0:T(128)}, u32[]{:S(2)}) copy-start(s32[17]{0:T(128)} %param.15) | copy-start | bytes 208
  115.4 101.1 %copy-start.7 = (s32[17]{0:T(128)S(1)}, s32[17]{0:T(128)}, u32[]{:S(2)}) copy-start(s32[17]{0:T(128)} %param.14) | copy-start | bytes 208
  115.4 342.7 %all-reduce.2.cloned.1.call-start = ((), (), s32[]{:S(2)}) async-start(), calls=%async_computation.6 | async-start | bytes 262144 | tf_op jit(solution)/shard_map/psum | solution.py:137
  215.1 412.5 %all-gather.2.cloned.1.call-start = ((), (), s32[]{:S(2)}) async-start(), calls=%async_computation.4 | async-start | bytes 2228224 | tf_op jit(solution)/shard_map/all_gather | solution.py:117
  218.0 11.8 %copy-start.4 = (s32[8192]{0:T(1024)}, s32[8192]{0:T(1024)S(1)}, u32[]{:S(2)}) copy-start(s32[8192]{0:T(1024)S(1)} %convert_reduce_fusion.1) | copy-start | bytes 98308
  233.0 3.0 copy-start.1
  404.4 66.7 %copy-start.6 = (s32[8192]{0:T(1024)S(1)}, s32[8192]{0:T(1024)}, u32[]{:S(2)}) copy-start(s32[8192]{0:T(1024)} %copy-done.5) | copy-start | bytes 98308
  465.2 155.4 %all-to-all-start.2 = ((f32[16,40,128]{2,1,0:T(8,128)}), f32[16,40,128]{2,1,0:T(8,128)}, u32[]{:S(2)}, u32[]{:S(2)}) async-start(f32[16,40,128]{2,1,0:T(8,128)} %get-tuple-element.45), calls=%async_computation.3 | async-start | bytes 655360 | tf_op jit(solution)/shard_map/all_to_all | solution.py:147
  504.1 6.4 copy-start.13
  510.4 45.5 %copy-start.9 = (s32[8192]{0:T(1024)S(1)}, s32[8192]{0:T(1024)}, u32[]{:S(2)}) copy-start(s32[8192]{0:T(1024)} %broadcast_clamp_fusion.2) | copy-start | bytes 98308
  556.0 50.9 %copy-start.10 = (s32[8192,1]{0,1:T(1,128)S(1)}, s32[8192,1]{0,1:T(1,128)}, u32[]{:S(2)}) copy-start(s32[8192,1]{0,1:T(1,128)} %get-tuple-element.36) | copy-start | bytes 98308
  556.0 51.9 %copy-start.12 = (s32[8192,1]{0,1:T(1,128)S(1)}, s32[8192,1]{0,1:T(1,128)}, u32[]{:S(2)}) copy-start(s32[8192,1]{0,1:T(1,128)} %get-tuple-element.82) | copy-start | bytes 98308
  556.0 51.9 %copy-start.15 = (pred[8192]{0:T(1024)(128)(4,1)S(1)}, pred[8192]{0:T(1024)(128)(4,1)}, u32[]{:S(2)}) copy-start(pred[8192]{0:T(1024)(128)(4,1)} %compare_reduce_fusion.20) | copy-start | bytes 24580
  556.0 51.9 %copy-start.16 = (pred[8192]{0:T(1024)(128)(4,1)S(1)}, pred[8192]{0:T(1024)(128)(4,1)}, u32[]{:S(2)}) copy-start(pred[8192]{0:T(1024)(128)(4,1)} %compare_reduce_fusion.21) | copy-start | bytes 24580
  556.0 51.9 %copy-start.17 = (pred[8192]{0:T(1024)(128)(4,1)S(1)}, pred[8192]{0:T(1024)(128)(4,1)}, u32[]{:S(2)}) copy-start(pred[8192]{0:T(1024)(128)(4,1)} %compare_reduce_fusion.22) | copy-start | bytes 24580
  556.0 51.9 %copy-start.18 = (pred[8192]{0:T(1024)(128)(4,1)S(1)}, pred[8192]{0:T(1024)(128)(4,1)}, u32[]{:S(2)}) copy-start(pred[8192]{0:T(1024)(128)(4,1)} %compare_reduce_fusion.23) | copy-start | bytes 24580
  556.1 51.9 %copy-start.19 = (pred[8192]{0:T(1024)(128)(4,1)S(1)}, pred[8192]{0:T(1024)(128)(4,1)}, u32[]{:S(2)}) copy-start(pred[8192]{0:T(1024)(128)(4,1)} %compare_reduce_fusion.24) | copy-start | bytes 24580
  556.1 51.9 %copy-start.20 = (pred[8192]{0:T(1024)(128)(4,1)S(1)}, pred[8192]{0:T(1024)(128)(4,1)}, u32[]{:S(2)}) copy-start(pred[8192]{0:T(1024)(128)(4,1)} %compare_reduce_fusion.25) | copy-start | bytes 24580
  556.1 51.9 %copy-start.21 = (pred[8192]{0:T(1024)(128)(4,1)S(1)}, pred[8192]{0:T(1024)(128)(4,1)}, u32[]{:S(2)}) copy-start(pred[8192]{0:T(1024)(128)(4,1)} %compare_reduce_fusion.26) | copy-start | bytes 24580
  556.1 51.9 %copy-start.22 = (pred[8192]{0:T(1024)(128)(4,1)S(1)}, pred[8192]{0:T(1024)(128)(4,1)}, u32[]{:S(2)}) copy-start(pred[8192]{0:T(1024)(128)(4,1)} %compare_reduce_fusion.27) | copy-start | bytes 24580
  556.1 51.9 %copy-start.23 = (pred[8192]{0:T(1024)(128)(4,1)S(1)}, pred[8192]{0:T(1024)(128)(4,1)}, u32[]{:S(2)}) copy-start(pred[8192]{0:T(1024)(128)(4,1)} %compare_reduce_fusion.28) | copy-start | bytes 24580
  556.1 51.9 %copy-start.24 = (pred[8192]{0:T(1024)(128)(4,1)S(1)}, pred[8192]{0:T(1024)(128)(4,1)}, u32[]{:S(2)}) copy-start(pred[8192]{0:T(1024)(128)(4,1)} %compare_reduce_fusion.29) | copy-start | bytes 24580
  556.1 58.2 %copy-start.3 = (s32[8192]{0:T(1024)S(1)}, s32[8192]{0:T(1024)}, u32[]{:S(2)}) copy-start(s32[8192]{0:T(1024)} %param.16) | copy-start | bytes 98308
  556.1 58.2 %copy-start.11 = (s32[8192,1]{0,1:T(1,128)S(1)}, s32[8192,1]{0,1:T(1,128)}, u32[]{:S(2)}) copy-start(s32[8192,1]{0,1:T(1,128)} %get-tuple-element.35) | copy-start | bytes 98308
  556.1 71.5 %copy-start.14 = (bf16[256,128]{1,0:T(8,128)(2,1)S(1)}, bf16[256,128]{1,0:T(8,128)(2,1)}, u32[]{:S(2)}) copy-start(bf16[256,128]{1,0:T(8,128)(2,1)} %param.12) | copy-start | bytes 196612
  556.1 71.5 %copy-start.26 = (f32[256]{0:T(256)S(1)}, f32[256]{0:T(256)}, u32[]{:S(2)}) copy-start(f32[256]{0:T(256)} %copy-done.25) | copy-start | bytes 3076
  620.7 140.4 %all-to-all-start = ((f32[16,40,128]{2,1,0:T(8,128)}), f32[16,40,128]{2,1,0:T(8,128)S(1)}, u32[]{:S(2)}, u32[]{:S(2)}) async-start(f32[16,40,128]{2,1,0:T(8,128)} %get-tuple-element.43), calls=%async_computation | async-start | bytes 655360 | tf_op jit(solution)/shard_map/all_to_all | solution.py:144
  715.5 49.7 %copy-start.28 = (bf16[8192,128]{1,0:T(8,128)(2,1)S(1)}, bf16[8192,128]{1,0:T(8,128)(2,1)}, u32[]{:S(2)}) copy-start(bf16[8192,128]{1,0:T(8,128)(2,1)} %all-gather.2.cloned.1.call-done) | copy-start | bytes 6291460
  761.1 16.9 %all-to-all-start.1 = ((f32[16,40,128]{2,1,0:T(8,128)}), f32[16,40,128]{2,1,0:T(8,128)S(1)}, u32[]{:S(2)}, u32[]{:S(2)}) async-start(f32[16,40,128]{2,1,0:T(8,128)} %get-tuple-element.44), calls=%async_computation.2 | async-start | bytes 655360 | tf_op jit(solution)/shard_map/all_to_all | solution.py:141
  773.6 6.0 copy-start.27
Sparse Core Ops, SparseCore 0:
  115.6 97.8 reduce-scatter.1
  216.3 17.4 all-reduce.1
  236.6 61.8 all-gather.1
